TPU v7x, 32 devices: a whole 2x2x4 slice. The times are simulated.
32 devices in a mesh: dp: 8 (over y, x, core), space: 4 (over z).
Axes of the slice: x: 2, y: 2, z: 4, core: 2. Of those that a mesh axis runs over, the one named last changes fastest.
Arguments:
- volume: bfloat16 [8, 8, 8, 8, 512], P('dp', 'space'), may hold values from -6 to 6
- conv_one: bfloat16 [3, 3, 3, 512, 256], P(None, None, None, 'dp'), may hold values from -0.125 to 0.125
- mix_one: bfloat16 [256, 256], P('dp'), may hold values from -0.375 to 0.375
- conv_two: bfloat16 [3, 3, 3, 256, 128], P(None, None, None, 'dp'), may hold values from -0.1875 to 0.1875
- mix_two: bfloat16 [128, 128], P('dp'), may hold values from -0.5 to 0.5
Outputs:
- decoded: bfloat16 [8, 32, 32, 32, 128], P('dp', 'space')
All inputs are finite; a program needn't handle non-finite values.
Results may differ from a plain program's by a relative error of at most 0.007.
Values may be sent and summed in bfloat16 or wider, within the bound.
A program may use at most 64 MiB of HBM per device.

v0:
```python
import jax
import jax.numpy as jnp
from jax import lax
from jax.sharding import PartitionSpec as P

PHASE_TAPS = (((1, 0),), ((2, 0), (0, 1)))


def shifted(block, axis, distance):
    devices = range(lax.axis_size(axis))
    route = [(i - distance, i) for i in devices if i - distance in devices]
    return lax.ppermute(block, axis, route)


def phase_sum(padded, weight, planes, height, breadth, depth_taps):
    chans_in = padded.shape[-1]
    chans_out = weight.shape[-1]
    groups = []
    for taps_depth in depth_taps:
        for taps_rows in PHASE_TAPS:
            for taps_cols in PHASE_TAPS:
                total = None
                for depth_tap, depth_shift in taps_depth:
                    for row_tap, row_shift in taps_rows:
                        for col_tap, col_shift in taps_cols:
                            piece = padded[
                                depth_shift : depth_shift + planes,
                                row_shift : row_shift + height,
                                col_shift : col_shift + breadth,
                            ]
                            term = jnp.dot(
                                piece.reshape(-1, chans_in),
                                weight[depth_tap, row_tap, col_tap],
                                preferred_element_type=jnp.float32,
                            )
                            total = term if total is None else total + term
                groups.append(total)
    return jnp.stack(groups).reshape(len(depth_taps), 2, 2, planes, height, breadth, chans_out)


def alternate(phased):
    planes, height, breadth, chans = phased.shape[3:]
    return jnp.transpose(phased, (3, 0, 4, 1, 5, 2, 6)).reshape(
        2 * planes, 2 * height, 2 * breadth, chans
    )


def expand(field, weight, first):
    planes, height, breadth, chans = field.shape
    if first:
        plane = shifted(field[0:1], "space", -1)
    else:
        plane = shifted(field[0:1], "space", -1)
    padded = jnp.pad(jnp.concatenate([field, plane], 0), ((0, 0), (0, 1), (0, 1), (0, 0)))
    phased = phase_sum(padded, weight, planes, height, breadth, PHASE_TAPS)
    return alternate(phased)


def finish(conv, mixing):
    act = jax.nn.silu(conv).astype(jnp.bfloat16)
    mixed = jnp.dot(act.reshape(-1, act.shape[-1]), mixing, preferred_element_type=jnp.float32)
    return mixed.astype(jnp.bfloat16).reshape(conv.shape[:-1] + (mixing.shape[1],))


def per_device(volume, conv_one, mix_one, conv_two, mix_two):
    field = volume[0]
    kernel_one, mixing_one = (
        lax.all_gather(conv_one, "dp", axis=3, tiled=True),
        lax.all_gather(mix_one, "dp", axis=0, tiled=True),
    )
    upper = finish(expand(field, kernel_one, True), mixing_one)
    kernel_two, mixing_two = (
        lax.all_gather(conv_two, "dp", axis=3, tiled=True),
        lax.all_gather(mix_two, "dp", axis=0, tiled=True),
    )
    decoded = finish(expand(upper, kernel_two, False), mixing_two)
    return decoded[None]


def solution(mesh):
    return jax.shard_map(
        per_device,
        mesh=mesh,
        in_specs=(
            P("dp", "space", None, None, None),
            P(None, None, None, "dp", None),
            P("dp", None),
            P(None, None, None, "dp", None),
            P("dp", None),
        ),
        out_specs=P("dp", "space", None, None, None),
        check_vma=False,
    )
```

profile of v0, /device:TPU:1, one launch (start us, length us, event | category | flops | bytes accessed | tf_op | source)
XLA Modules:
  0.0 114.6 jit_solution(14823665278782194715)
XLA Ops:
  6.5 0.7 all-gather.3.cloned.1.call-update
  7.3 0.8 slice_bitcast_fusion.108
  8.2 1.3 %collective-permute-start = (bf16[1,8,8,512]{3,2,1,0:T(8,128)(2,1)S(1)}, bf16[1,8,8,512]{3,2,1,0:T(8,128)(2,1)S(1)}, u32[]{:S(2)}, u32[]{:S(2)}) collective-permute-start(bf16[1,8,8,512]{3,2,1,0:T(8,128)(2,1)S(1)} %slice_bitcast_fusion.108), channel_id=1, source_target_pairs={{1,0},{2,1},{3,2},{5,4},{6,5},{7,6},{9,8},{10,9},{11,10},{13,12},{... | collective-permute-start | bytes 196616 | tf_op jit(solution)/shard_map/ppermute | solution.py:12
  9.5 10.5 %all_gather.15 = bf16[128,128]{1,0:T(8,128)(2,1)S(1)} all-gather(bf16[16,128]{1,0:T(8,128)(2,1)} %param.9), channel_id=1, replica_groups=mesh['dp'=8,'space'=4] {'dp'}, dimensions={0}, use_global_device_ids=true | all-gather | bytes 36864 | tf_op jit(solution)/shard_map/all_gather | solution.py:74
  20.0 9.4 %all_gather.13 = bf16[256,256]{1,0:T(8,128)(2,1)S(1)} all-gather(bf16[32,256]{1,0:T(8,128)(2,1)} %param.7), channel_id=1, replica_groups=mesh['dp'=8,'space'=4] {'dp'}, dimensions={0}, use_global_device_ids=true | all-gather | bytes 147456 | tf_op jit(solution)/shard_map/all_gather | solution.py:69
  29.4 0.9 pad_maximum_fusion.1
  30.4 0.9 fusion.38
  31.2 29.9 %all-gather.3.cloned.1.call-done = bf16[3,3,3,512,256]{4,3,2,1,0:T(8,128)(2,1)} async-done(((bf16[3,3,3,64,256]{4,3,2,1,0:T(8,128)(2,1)}), bf16[3,3,3,512,256]{4,3,2,1,0:T(8,128)(2,1)}) %all-gather.3.cloned.1.call-update) | async-done | bytes 7077904 | tf_op jit(solution)/shard_map/all_gather | solution.py:68
  61.2 1.4 %fusion.29 = f32[8,128,256]{2,1,0:T(8,128)S(1)} fusion(bf16[128,512]{1,0:T(8,128)(2,1)} %bitcast.315, bf16[3,3,3,512,256]{4,3,2,1,0:T(8,128)(2,1)} %all-gather.3.cloned.1.call-done), kind=kOutput, calls=%fused_computation.78 | convolution fusion | flops 33554432 | bytes 524288 | tf_op jit(solution)/shard_map/dot_general | solution.py:31
  62.5 1.5 %fusion.37 = f32[128,256]{1,0:T(8,128)S(1)} fusion(bf16[128,512]{1,0:T(8,128)(2,1)} %bitcast.316, bf16[3,3,3,512,256]{4,3,2,1,0:T(8,128)(2,1)} %all-gather.3.cloned.1.call-done), kind=kOutput, calls=%fused_computation.123 | convolution fusion | flops 33554432 | bytes 524288 | tf_op jit(solution)/shard_map/dot_general | solution.py:31
  64.0 1.1 fusion.36
  65.2 1.1 fusion.35
  66.3 1.1 fusion.33
  67.5 1.1 fusion.32
  68.6 1.1 fusion.31
  69.8 1.1 %convolution_add_fusion.35 = f32[128,256]{1,0:T(8,128)S(1)} fusion(f32[128,256]{1,0:T(8,128)S(1)} %fusion.35, bf16[128,512]{1,0:T(8,128)(2,1)S(1)} %bitcast.352, bf16[3,3,3,512,256]{4,3,2,1,0:T(8,128)(2,1)} %all-gather.3.cloned.1.call-done), kind=kOutput, calls=%fused_computation.70 | convolution fusion | flops 33587200 | bytes 655360 | tf_op jit(solution)/shard_map/dot_general | solution.py:31
  70.9 1.2 %convolution_add_fusion.31 = f32[128,256]{1,0:T(8,128)S(1)} fusion(f32[128,256]{1,0:T(8,128)S(1)} %fusion.33, bf16[128,512]{1,0:T(8,128)(2,1)S(1)} %bitcast.353, bf16[3,3,3,512,256]{4,3,2,1,0:T(8,128)(2,1)} %all-gather.3.cloned.1.call-done), kind=kOutput, calls=%fused_computation.62 | convolution fusion | flops 33587200 | bytes 655360 | tf_op jit(solution)/shard_map/dot_general | solution.py:31
  72.1 1.1 convolution_add_fusion.34
  73.2 1.1 convolution_add_fusion.28
  74.4 1.1 convolution_add_fusion.30
  75.5 1.1 convolution_add_fusion.27
  79.5 0.8 copy.9
  80.3 0.7 reshape.55
  81.0 0.4 convolution_convert_fusion.1
  81.5 1.5 %collective-permute-start.1 = (bf16[1,16,16,256]{3,2,1,0:T(8,128)(2,1)S(1)}, bf16[1,16,16,256]{3,2,1,0:T(8,128)(2,1)S(1)}, u32[]{:S(2)}, u32[]{:S(2)}) collective-permute-start(bf16[1,16,16,256]{3,2,1,0:T(8,128)(2,1)S(1)} %bitcast.365), channel_id=1, source_target_pairs={{1,0},{2,1},{3,2},{5,4},{6,5},{7,6},{9,8},{10,9},{11,10},{13,12},{... | collective-permute-start | bytes 393224 | tf_op jit(solution)/shard_map/ppermute | solution.py:12
  82.9 6.9 %all-gather.5.cloned.1.call-done = bf16[3,3,3,256,128]{4,3,2,1,0:T(8,128)(2,1)} async-done(((bf16[3,3,3,32,128]{4,3,2,1,0:T(8,128)(2,1)}), bf16[3,3,3,256,128]{4,3,2,1,0:T(8,128)(2,1)}) %all-gather.5.cloned.1.call-update) | async-done | bytes 1769488 | tf_op jit(solution)/shard_map/all_gather | solution.py:73
  89.9 1.3 %fusion = f32[8,1024,128]{2,1,0:T(8,128)S(1)} fusion(bf16[1024,256]{1,0:T(8,128)(2,1)S(1)} %convolution_convert_fusion.1, bf16[3,3,3,256,128]{4,3,2,1,0:T(8,128)(2,1)} %all-gather.5.cloned.1.call-done), kind=kOutput, calls=%fused_computation.10 | convolution fusion | flops 67108864 | bytes 1114112 | tf_op jit(solution)/shard_map/dot_general | solution.py:31
  91.1 1.1 fusion.45
  92.3 1.1 fusion.44
  93.4 1.1 fusion.43
  102.0 3.3 %copy.7 = f32[2,2,2,4,16,16,128]{6,2,5,1,4,0,3:T(2,128)S(1)} copy(f32[2,2,2,4,16,16,128]{6,5,4,3,2,1,0:T(8,128)S(1)} %bitcast.335) | data formatting | bytes 8388608 | tf_op jit(solution)/shard_map/reshape | solution.py:38
  105.2 2.5 %convolution_convert_fusion = bf16[8192,128]{1,0:T(8,128)(2,1)} fusion(bf16[128,128]{1,0:T(8,128)(2,1)S(1)} %all_gather.15, f32[8192,128]{1,0:T(8,128)S(1)} %bitcast.342), kind=kOutput, calls=%fused_computation | convolution fusion | flops 274726912 | bytes 6324224 | tf_op jit(solution)/shard_map/dot_general | solution.py:61
  (53 shorter events, 10.1 us)
Async XLA Ops:
  6.5 57.5 %copy-start = (bf16[1,2,8,8,512]{4,3,2,1,0:T(8,128)(2,1)S(1)}, bf16[1,2,8,8,512]{4,3,2,1,0:T(8,128)(2,1)}, u32[]{:S(2)}) copy-start(bf16[1,2,8,8,512]{4,3,2,1,0:T(8,128)(2,1)} %param.5) | copy-start | bytes 393220
  6.5 54.6 %all-gather.3.cloned.1.call-start = ((), (), s32[]{:S(2)}) async-start(), calls=%async_computation | async-start | bytes 7962624 | tf_op jit(solution)/shard_map/all_gather | solution.py:68
  7.3 82.6 %all-gather.5.cloned.1.call-start = ((), (), s32[]{:S(2)}) async-start(), calls=%async_computation.1 | async-start | bytes 1990656 | tf_op jit(solution)/shard_map/all_gather | solution.py:73
  8.2 21.2 %collective-permute-start = (bf16[1,8,8,512]{3,2,1,0:T(8,128)(2,1)S(1)}, bf16[1,8,8,512]{3,2,1,0:T(8,128)(2,1)S(1)}, u32[]{:S(2)}, u32[]{:S(2)}) collective-permute-start(bf16[1,8,8,512]{3,2,1,0:T(8,128)(2,1)S(1)} %slice_bitcast_fusion.108), channel_id=1, source_target_pairs={{1,0},{2,1},{3,2},{5,4},{6,5},{7,6},{9,8},{10,9},{11,10},{13,12},{... | collective-permute-start | bytes 196616 | tf_op jit(solution)/shard_map/ppermute | solution.py:12
  61.2 15.5 %copy-start.1 = (bf16[3,3,3,512,256]{4,3,2,1,0:T(8,128)(2,1)S(1)}, bf16[3,3,3,512,256]{4,3,2,1,0:T(8,128)(2,1)}, u32[]{:S(2)}) copy-start(bf16[3,3,3,512,256]{4,3,2,1,0:T(8,128)(2,1)} %all-gather.3.cloned.1.call-done) | copy-start | bytes 21233668
  81.5 14.3 %collective-permute-start.1 = (bf16[1,16,16,256]{3,2,1,0:T(8,128)(2,1)S(1)}, bf16[1,16,16,256]{3,2,1,0:T(8,128)(2,1)S(1)}, u32[]{:S(2)}, u32[]{:S(2)}) collective-permute-start(bf16[1,16,16,256]{3,2,1,0:T(8,128)(2,1)S(1)} %bitcast.365), channel_id=1, source_target_pairs={{1,0},{2,1},{3,2},{5,4},{6,5},{7,6},{9,8},{10,9},{11,10},{13,12},{... | collective-permute-start | bytes 393224 | tf_op jit(solution)/shard_map/ppermute | solution.py:12
  89.9 4.7 %copy-start.2 = (bf16[3,3,3,256,128]{4,3,2,1,0:T(8,128)(2,1)S(1)}, bf16[3,3,3,256,128]{4,3,2,1,0:T(8,128)(2,1)}, u32[]{:S(2)}) copy-start(bf16[3,3,3,256,128]{4,3,2,1,0:T(8,128)(2,1)} %all-gather.5.cloned.1.call-done) | copy-start | bytes 5308420
Sparse Core Ops, SparseCore 0:
  9.3 51.8 all-gather.2
  63.1 26.7 all-gather.4
where the time goes:
time: 116 us; the launch traced here: 115 us
  waiting for transfers between devices  37.6 us (32%)
  matrix products  32.5 us (28%)
  blocking collectives  19.9 us (17%)
  between operations  13.9 us (12%)
  local copies, waits for them, and re-layouts  6.06 us (5%)
  starting transfers between devices  2.79 us (2%)
  other arithmetic  1.89 us (2%)
    all_gather x1, waiting for transfers between devices, per_device(): lax.all_gather(conv_one, 'dp', axis=3, tiled=True)  29.9 us
    dot_general x54, matrix products, phase_sum(): jnp.dot(piece.reshape(-1, chans_in), weight[depth_tap, row_tap, col_tap],...  29.5 us
    all_gather x1, blocking collectives, per_device(): lax.all_gather(mix_two, 'dp', axis=0, tiled=True)  10.5 us
    all_gather x1, blocking collectives, per_device(): lax.all_gather(mix_one, 'dp', axis=0, tiled=True)  9.38 us
    all_gather x1, waiting for transfers between devices, per_device(): lax.all_gather(conv_two, 'dp', axis=3, tiled=True)  6.94 us
    reshape x2, local copies, waits for them, and re-layouts, phase_sum(): jnp.stack(groups)  4.09 us
    dot_general x2, matrix products, finish(): jnp.dot(act.reshape(-1, act.shape[-1]), mixing, preferred_element_type=jn...  2.96 us
    ppermute x2, starting transfers between devices, shifted(): return lax.ppermute(block, axis, route)  2.75 us
  transfers between devices with their start and end apart: 4, of which 2 were waited for; matrix products, arithmetic and copies ran while one was open for 25% of the time, Pallas kernels for 0%

commit v1 on v0

v1 whole, which is shorter than its diff:
```python
import functools

import jax
import jax.numpy as jnp
from jax import lax
from jax.experimental import pallas as pl
from jax.experimental.pallas import tpu as pltpu
from jax.sharding import PartitionSpec as P

MESH = pl.DeviceIdType.MESH
BF = jnp.bfloat16
F32 = jnp.float32
PHASE_TAPS = (((1, 0),), ((2, 0), (0, 1)))
DEPTH_TAPS = (1, 2, 0)


def taps_of(pd, pr, pc):
    for kd, sd in PHASE_TAPS[pd]:
        for kr, sr in PHASE_TAPS[pr]:
            for kc, sc in PHASE_TAPS[pc]:
                yield kd * 9 + kr * 3 + kc, sd * 4 + sr * 2 + sc


def silu(v):
    return v / (1.0 + jnp.exp(-v))


def first_kernel(
    n_dp, n_space, vol, w1, m1, w2, m2,
    up, w2all, m2all,
    gat, m1all, m1s, volx, pad, xs, act_all, act_in, upf, halo,
    ssem, rsem, fssem, frsem, vs, vr, hs, hr, asem, arsem, us, ur,
):
    n = n_dp // 2
    me = lax.axis_index("dp")
    s = lax.axis_index("space")
    q, core = me // 2, lax.rem(me, 2)
    sib = q * 2 + (1 - core)
    h = lax.rem(s, 2)
    mate = s + 1 - 2 * h
    base = s - h

    def peer(k):
        return lax.rem(q + k, n) * 2 + core

    def source(k):
        return lax.rem(q + n - k, n) * 2 + core

    def sib_source(k):
        return lax.rem(q + n - k, n) * 2 + (1 - core)

    barrier = pltpu.get_barrier_semaphore()
    for k in range(1, n):
        pl.semaphore_signal(barrier, inc=1, device_id={"dp": peer(k)}, device_id_type=MESH)
    pl.semaphore_signal(barrier, inc=1, device_id={"dp": sib}, device_id_type=MESH)
    for k in range(1, n_space):
        pl.semaphore_signal(
            barrier, inc=1, device_id={"space": lax.rem(s + k, n_space)}, device_id_type=MESH
        )
    pl.semaphore_wait(barrier, n + n_space - 1)

    lanes = pl.ds(pl.multiple_of(h * 128, 128), 128)

    def ends(item, slot):
        if item < 3:
            rows = pl.ds(DEPTH_TAPS[item] * 9, 9)
            return w1.at[rows, :, lanes], gat.at[slot, rows]
        mine, every = ((m1, m1all), (w2, w2all), (m2, m2all))[item - 3]
        return mine, every.at[slot]

    def to_peer(item, k):
        src, dst = ends(item, me)
        return pltpu.make_async_remote_copy(
            src, dst, ssem.at[item, k], rsem.at[item, k],
            device_id={"dp": peer(k)}, device_id_type=MESH,
        )

    def to_sib(item, k):
        if k == 0:
            src, dst = ends(item, me)
        else:
            _, dst = ends(item, source(k))
            src = dst
        return pltpu.make_async_remote_copy(
            src, dst, fssem.at[item, k], frsem.at[item, k],
            device_id={"dp": sib}, device_id_type=MESH,
        )

    def send(item):
        for k in range(1, n):
            to_peer(item, k).start()
        to_sib(item, 0).start()

    def forward(item):
        for k in range(1, n):
            to_peer(item, k).wait_recv()
            to_sib(item, k).start()

    def settle(item):
        for k in range(n):
            to_sib(item, k).wait_recv()

    def to_mate():
        return pltpu.make_async_remote_copy(
            vol, volx.at[pl.ds(2 * h, 2)], vs.at[0], vr.at[0],
            device_id={"space": mate}, device_id_type=MESH,
        )

    def vol_halo(j):
        return pltpu.make_async_remote_copy(
            vol.at[pl.ds(0, 1)], volx.at[pl.ds(4, 1)], hs.at[j], hr.at[0],
            device_id={"space": s - 1 - j}, device_id_type=MESH,
        )

    gives = jnp.logical_and(h == 0, s >= 2)
    takes = base + 2 < n_space

    to_mate().start()

    @pl.when(gives)
    def _():
        vol_halo(0).start()
        vol_halo(1).start()

    for item in (0, 3, 1, 2):
        send(item)

    gat[me] = w1[:, :, lanes]
    m1all[me] = m1[...]
    w2all[me] = w2[...]
    m2all[me] = m2[...]
    volx[pl.ds(2 * h, 2)] = vol[...]

    to_mate().wait_recv()

    @pl.when(takes)
    def _():
        vol_halo(0).wait_recv()

    @pl.when(jnp.logical_not(takes))
    def _():
        volx[pl.ds(4, 1)] = jnp.zeros((1,) + volx.shape[1:], BF)

    pad[:, :, 8:9] = jnp.zeros((2, 5, 1) + pad.shape[3:], F32)
    x = volx[...].astype(F32)
    pad[0, :, 0:8] = x
    pad[1, :, 0:8] = jnp.concatenate([x[:, :, 1:], jnp.zeros_like(x[:, :, :1])], 2)
    for sd in range(2):
        for sr in range(2):
            for sc in range(2):
                v = pad[sc, sd : sd + 4, sr : sr + 8]
                xs[sd * 4 + sr * 2 + sc] = v.reshape(256, v.shape[-1]).astype(BF)

    def to_act(p):
        return pltpu.make_async_remote_copy(
            act_all.at[p, 1 - h], act_in.at[p], asem.at[p], arsem.at[p],
            device_id={"space": mate}, device_id_type=MESH,
        )

    def conv_phase(p):
        acc = None
        for t, sh in taps_of(p // 4, p // 2 % 2, p % 2):
            w = gat[:, t].reshape(-1, 128)
            term = jnp.dot(xs[sh], w, preferred_element_type=F32)
            acc = term if acc is None else acc + term
        act_all[p] = silu(acc).astype(BF).reshape(2, 128, 128)
        to_act(p).start()

    def mix_phase(p):
        pd, pr, pc = p // 4, p // 2 % 2, p % 2
        to_act(p).wait_recv()
        r = jnp.dot(act_all[p, h], m1s[h], preferred_element_type=F32)
        r = r + jnp.dot(act_in[p], m1s[1 - h], preferred_element_type=F32)
        for d in range(2):
            for i in range(8):
                row = d * 64 + i * 8
                for half in range(2):
                    upf[2 * d + pd, 2 * i + pr, half, pl.ds(pc, 8, stride=2), :] = r[
                        row : row + 8, half * 128 : half * 128 + 128
                    ]

    forward(0)
    forward(3)
    settle(0)
    for p in range(4):
        conv_phase(p)
    forward(1)
    forward(2)
    send(4)
    send(5)
    settle(3)
    m1s[...] = m1all[...].reshape(2, 128, 256)
    for p in range(4):
        mix_phase(p)

    def emit(plane):
        for half in range(2):
            up[plane, 0:16, :, half * 128 : half * 128 + 128] = upf[plane, :, half].astype(BF)

    emit(0)

    def up_halo():
        return pltpu.make_async_remote_copy(
            up.at[0, pl.ds(0, 16)], halo, us.at[0], ur.at[0],
            device_id={"space": s - 1}, device_id_type=MESH,
        )

    @pl.when(s > 0)
    def _():
        up_halo().start()

    settle(1)
    settle(2)
    for p in range(4, 8):
        conv_phase(p)
    forward(4)
    forward(5)
    for p in range(4, 8):
        mix_phase(p)
    for plane in range(1, 4):
        emit(plane)
    up[:, 16:17] = jnp.zeros((5, 1) + up.shape[2:], BF)

    last = s + 1 == n_space

    @pl.when(last)
    def _():
        up[4, 0:16] = jnp.zeros(halo.shape, BF)

    @pl.when(jnp.logical_not(last))
    def _():
        up_halo().wait_recv()
        up[4, 0:16] = halo[...]

    settle(4)
    settle(5)
    for item in range(6):
        for k in range(n):
            if k:
                to_peer(item, k).wait_send()
            to_sib(item, k).wait_send()
    to_mate().wait_send()
    for p in range(8):
        to_act(p).wait_send()

    @pl.when(gives)
    def _():
        vol_halo(0).wait_send()
        vol_halo(1).wait_send()

    @pl.when(s > 0)
    def _():
        up_halo().wait_send()


def second_kernel(up, w2, m2, out, wide, xs):
    d = pl.program_id(0)
    for sd in range(2):
        x = up[d + sd]
        moved = x.astype(F32)
        moved = jnp.concatenate([moved[:, 1:], jnp.zeros_like(moved[:, :1])], 1).astype(BF)
        for sr in range(2):
            xs[sd * 4 + sr * 2] = x[sr : sr + 16].reshape(256, 256)
            xs[sd * 4 + sr * 2 + 1] = moved[sr : sr + 16].reshape(256, 256)
    mixing = m2[...].reshape(128, 128)
    for p in range(8):
        pd, pr, pc = p // 4, p // 2 % 2, p % 2
        acc = None
        for t, sh in taps_of(pd, pr, pc):
            term = jnp.dot(xs[sh], w2[:, t].reshape(256, 128), preferred_element_type=F32)
            acc = term if acc is None else acc + term
        r = jnp.dot(silu(acc).astype(BF), mixing, preferred_element_type=F32)
        for i in range(16):
            wide[pd, 2 * i + pr, pl.ds(pc, 16, stride=2), :] = r[i * 16 : i * 16 + 16]
    out[...] = wide[...].astype(BF)


def per_device(n_dp, n_space, volume, conv_one, mix_one, conv_two, mix_two):
    n = n_dp // 2
    w1 = conv_one.reshape((27,) + conv_one.shape[3:])
    w2 = conv_two.reshape((27,) + conv_two.shape[3:])
    vm = pl.BlockSpec(memory_space=pltpu.VMEM)
    dma = pltpu.SemaphoreType.DMA
    up, w2all, m2all = pl.pallas_call(
        functools.partial(first_kernel, n_dp, n_space),
        out_shape=(
            jax.ShapeDtypeStruct((5, 17, 16, 256), BF),
            jax.ShapeDtypeStruct((n_dp,) + w2.shape, BF),
            jax.ShapeDtypeStruct((n_dp,) + mix_two.shape, BF),
        ),
        in_specs=[vm] * 5,
        out_specs=(vm,) * 3,
        scratch_shapes=[
            pltpu.VMEM((n_dp, 27, w1.shape[1], 128), BF),
            pltpu.VMEM((n_dp,) + mix_one.shape, BF),
            pltpu.VMEM((2, 128, 256), BF),
            pltpu.VMEM((5, 8, 8, 512), BF),
            pltpu.VMEM((2, 5, 9, 8, 512), F32),
            pltpu.VMEM((8, 256, 512), BF),
            pltpu.VMEM((8, 2, 128, 128), BF),
            pltpu.VMEM((8, 128, 128), BF),
            pltpu.VMEM((4, 16, 2, 16, 128), F32),
            pltpu.VMEM((16, 16, 256), BF),
            dma((6, n)), dma((6, n)), dma((6, n)), dma((6, n)),
            dma((1,)), dma((1,)), dma((2,)), dma((1,)),
            dma((8,)), dma((8,)), dma((1,)), dma((1,)),
        ],
        compiler_params=pltpu.CompilerParams(
            collective_id=0, has_side_effects=True, vmem_limit_bytes=48 * 2**20
        ),
    )(volume[0], w1, mix_one, w2, mix_two)
    whole = lambda shape: pl.BlockSpec(shape, lambda d: (0,) * len(shape))
    decoded = pl.pallas_call(
        second_kernel,
        grid=(4,),
        out_shape=jax.ShapeDtypeStruct((8, 32, 32, 128), BF),
        in_specs=[whole(up.shape), whole(w2all.shape), whole(m2all.shape)],
        out_specs=pl.BlockSpec((2, 32, 32, 128), lambda d: (d, 0, 0, 0)),
        scratch_shapes=[pltpu.VMEM((2, 32, 32, 128), F32), pltpu.VMEM((8, 256, 256), BF)],
        compiler_params=pltpu.CompilerParams(vmem_limit_bytes=40 * 2**20),
    )(up, w2all, m2all)
    return decoded[None]


def solution(mesh):
    return jax.shard_map(
        functools.partial(per_device, mesh.shape["dp"], mesh.shape["space"]),
        mesh=mesh,
        in_specs=(
            P("dp", "space", None, None, None),
            P(None, None, None, "dp", None),
            P("dp", None),
            P(None, None, None, "dp", None),
            P("dp", None),
        ),
        out_specs=P("dp", "space", None, None, None),
        check_vma=False,
    )
```

time: 116 us -> 54.4 us (0.47)
  Pallas kernels: 0 us -> 49.7 us
  waiting for transfers between devices: 37.6 us -> 0 us
  matrix products: 32.5 us -> 0 us
  blocking collectives: 19.9 us -> 0 us
  between operations: 13.9 us -> 0.01 us
  starting transfers between devices: 2.79 us -> 0 us
  other arithmetic: 1.89 us -> 0 us
  local copies, waits for them, and re-layouts: 6.06 us -> 4.41 us
    pallas_call x0 -> x2, Pallas kernels: none -> 49.7 us  [the longest x1 39.9 us: per_device(): pl.pallas_call(functools.partial(first_kernel, n_dp, n_space), out_shape=...]
    all_gather x2 -> x0, waiting for transfers between devices: 36.9 us -> none  [the longest x1 29.9 us: per_device(): lax.all_gather(conv_one, 'dp', axis=3, tiled=True)]
    dot_general x56 -> x0, matrix products: 32.5 us -> none  [the longest x54 29.5 us: phase_sum(): jnp.dot(piece.reshape(-1, chans_in), weight[depth_tap, row_tap, col_tap],...]
    all_gather x2 -> x0, blocking collectives: 19.9 us -> none  [the longest x1 10.5 us: per_device(): lax.all_gather(mix_two, 'dp', axis=0, tiled=True)]
    reshape x3 -> x0, local copies, waits for them, and re-layouts: 4.81 us -> none  [the longest x2 4.09 us: phase_sum(): jnp.stack(groups)]
    unnamed x6 -> x10, local copies, waits for them, and re-layouts: 0.01 us -> 4.41 us
    ppermute x2 -> x0, starting transfers between devices: 2.75 us -> none  [shifted(): return lax.ppermute(block, axis, route)]
    concatenate x4 -> x0, other arithmetic: 1.89 us -> none  [expand(): jnp.concatenate([field, plane], 0)]
  transfers between devices with their start and end apart: 4 -> 0, of which waited for: 2 -> 0; matrix products, arithmetic and copies ran while one was open for 25% -> 0% of each run, Pallas kernels for 0% -> 0%
where the time goes in v1:
time: 54.4 us; the launch traced here: 54.1 us
  Pallas kernels  49.7 us (91%)
  local copies, waits for them, and re-layouts  4.41 us (8%)
    pallas_call x1, Pallas kernels, per_device(): pl.pallas_call(functools.partial(first_kernel, n_dp, n_space), out_shape=...  39.9 us
    pallas_call x1, Pallas kernels, per_device(): pl.pallas_call(second_kernel, grid=(4,), out_shape=jax.ShapeDtypeStruct((...  9.74 us
    unnamed x10, local copies, waits for them, and re-layouts  4.41 us

profile of v1, /device:TPU:1, one launch (start us, length us, event | category | flops | bytes accessed | tf_op | source)
XLA Modules:
  0.0 54.1 jit_solution(5807623963904829353)
XLA Ops:
  0.0 0.0 copy-start
  0.0 1.2 %copy-done = bf16[3,3,3,64,256]{4,3,2,1,0:T(8,128)(2,1)S(1)} copy-done((bf16[3,3,3,64,256]{4,3,2,1,0:T(8,128)(2,1)S(1)}, bf16[3,3,3,64,256]{4,3,2,1,0:T(8,128)(2,1)}, u32[]{:S(2)}) %copy-start) | copy-done | bytes 884760
  1.2 0.0 copy-start.1
  1.2 0.9 %copy-done.1 = bf16[3,3,3,32,128]{4,3,2,1,0:T(8,128)(2,1)S(1)} copy-done((bf16[3,3,3,32,128]{4,3,2,1,0:T(8,128)(2,1)S(1)}, bf16[3,3,3,32,128]{4,3,2,1,0:T(8,128)(2,1)}, u32[]{:S(2)}) %copy-start.1) | copy-done | bytes 221208
  2.1 0.0 copy-start.2
  2.1 0.9 %copy-done.2 = bf16[1,2,8,8,512]{4,3,2,1,0:T(8,128)(2,1)S(1)} copy-done((bf16[1,2,8,8,512]{4,3,2,1,0:T(8,128)(2,1)S(1)}, bf16[1,2,8,8,512]{4,3,2,1,0:T(8,128)(2,1)}, u32[]{:S(2)}) %copy-start.2) | copy-done | bytes 131096
  3.0 0.0 copy-start.3
  3.0 0.7 %copy-done.3 = bf16[32,256]{1,0:T(8,128)(2,1)S(1)} copy-done((bf16[32,256]{1,0:T(8,128)(2,1)S(1)}, bf16[32,256]{1,0:T(8,128)(2,1)}, u32[]{:S(2)}) %copy-start.3) | copy-done | bytes 16408
  3.7 0.0 copy-start.4
  3.7 0.7 %copy-done.4 = bf16[16,128]{1,0:T(8,128)(2,1)S(1)} copy-done((bf16[16,128]{1,0:T(8,128)(2,1)S(1)}, bf16[16,128]{1,0:T(8,128)(2,1)}, u32[]{:S(2)}) %copy-start.4) | copy-done | bytes 4120
  4.4 39.9 %shard_map.55 = (bf16[5,17,16,256]{3,2,1,0:T(8,128)(2,1)S(1)}, bf16[8,27,32,128]{3,2,1,0:T(8,128)(2,1)S(1)}, bf16[8,16,128]{2,1,0:T(8,128)(2,1)S(1)}) custom-call(bf16[2,8,8,512]{3,2,1,0:T(8,128)(2,1)S(1)} %bitcast.6, bf16[27,64,256]{2,1,0:T(8,128)(2,1)S(1)} %bitcast.4, bf16[32,256]{1,0:T(8,128)(2,1)S(1)} %copy-done.3, bf16[27,32,128]{2,1,0:T(8,128)(2,1)S(1)} %bitcast.5, ...), custom_call_target="tpu_custom_call" | custom-call | tf_op jit(solution)/shard_map/pallas_call | solution.py:284
  44.3 9.7 %shard_map.56 = bf16[8,32,32,128]{3,2,1,0:T(8,128)(2,1)} custom-call(bf16[5,17,16,256]{3,2,1,0:T(8,128)(2,1)S(1)} %get-tuple-element.8.up, bf16[8,27,32,128]{3,2,1,0:T(8,128)(2,1)S(1)} %get-tuple-element.9.w2, bf16[8,16,128]{2,1,0:T(8,128)(2,1)S(1)} %get-tuple-element.10.m2), custom_call_target="tpu_custom_call" | custom-call | tf_op jit(solution)/shard_map/pallas_call | solution.py:313
Async XLA Ops:
  0.0 1.2 %copy-start = (bf16[3,3,3,64,256]{4,3,2,1,0:T(8,128)(2,1)S(1)}, bf16[3,3,3,64,256]{4,3,2,1,0:T(8,128)(2,1)}, u32[]{:S(2)}) copy-start(bf16[3,3,3,64,256]{4,3,2,1,0:T(8,128)(2,1)} %param.6) | copy-start | bytes 2654212
  1.2 0.9 %copy-start.1 = (bf16[3,3,3,32,128]{4,3,2,1,0:T(8,128)(2,1)S(1)}, bf16[3,3,3,32,128]{4,3,2,1,0:T(8,128)(2,1)}, u32[]{:S(2)}) copy-start(bf16[3,3,3,32,128]{4,3,2,1,0:T(8,128)(2,1)} %param.8) | copy-start | bytes 663556
  2.1 0.9 %copy-start.2 = (bf16[1,2,8,8,512]{4,3,2,1,0:T(8,128)(2,1)S(1)}, bf16[1,2,8,8,512]{4,3,2,1,0:T(8,128)(2,1)}, u32[]{:S(2)}) copy-start(bf16[1,2,8,8,512]{4,3,2,1,0:T(8,128)(2,1)} %param.5) | copy-start | bytes 393220
  3.0 0.7 %copy-start.3 = (bf16[32,256]{1,0:T(8,128)(2,1)S(1)}, bf16[32,256]{1,0:T(8,128)(2,1)}, u32[]{:S(2)}) copy-start(bf16[32,256]{1,0:T(8,128)(2,1)} %m1.1) | copy-start | bytes 49156
  3.7 0.7 %copy-start.4 = (bf16[16,128]{1,0:T(8,128)(2,1)S(1)}, bf16[16,128]{1,0:T(8,128)(2,1)}, u32[]{:S(2)}) copy-start(bf16[16,128]{1,0:T(8,128)(2,1)} %m2.1) | copy-start | bytes 12292

commit v2 on v1

--- a/solution.py
+++ b/solution.py
@@ -14,22 +14,29 @@
 DEPTH_TAPS = (1, 2, 0)
 
 
-def taps_of(pd, pr, pc):
+def silu(v):
+    u = 0.5 * v
+    return u + u * jnp.tanh(u)
+
+
+def pair_sum(xs, weight, pd, pr):
+    both, extra = None, None
     for kd, sd in PHASE_TAPS[pd]:
         for kr, sr in PHASE_TAPS[pr]:
-            for kc, sc in PHASE_TAPS[pc]:
-                yield kd * 9 + kr * 3 + kc, sd * 4 + sr * 2 + sc
-
-
-def silu(v):
-    return v / (1.0 + jnp.exp(-v))
+            t, sh = kd * 9 + kr * 3, sd * 4 + sr * 2
+            wide = jnp.concatenate([weight(t + 1), weight(t + 2)], 1)
+            a = jnp.dot(xs[sh], wide, preferred_element_type=F32)
+            b = jnp.dot(xs[sh + 1], weight(t), preferred_element_type=F32)
+            both = a if both is None else both + a
+            extra = b if extra is None else extra + b
+    return both[:, :128], both[:, 128:] + extra
 
 
 def first_kernel(
     n_dp, n_space, vol, w1, m1, w2, m2,
     up, w2all, m2all,
     gat, m1all, m1s, volx, pad, xs, act_all, act_in, upf, halo,
-    ssem, rsem, fssem, frsem, vs, vr, hs, hr, asem, arsem, us, ur,
+    ssem, rsem, fssem, frsem, vs, vr, hs, hr, asem, arsem, us, ur, own,
 ):
     n = n_dp // 2
     me = lax.axis_index("dp")
@@ -86,19 +93,76 @@
             device_id={"dp": sib}, device_id_type=MESH,
         )
 
+    flip = {
+        1: q + 1 - 2 * lax.rem(q, 2),
+        2: q + 2 - 4 * lax.rem(q // 2, 2),
+    }
+
+    def crosses(item):
+        return n == 4 and item in (0, 1, 2, 4)
+
+    def straight(item, k):
+        src, dst = ends(item, me)
+        return pltpu.make_async_remote_copy(
+            src, dst, ssem.at[item, k], rsem.at[item, k],
+            device_id={"dp": flip[k] * 2 + core}, device_id_type=MESH,
+        )
+
+    def half_of(item, chip, j):
+        slot = chip * 2 + core
+        if item < 3:
+            rows = gat.shape[2] // 2
+            return gat.at[slot, pl.ds(DEPTH_TAPS[item] * 9, 9), pl.ds(j * rows, rows)]
+        return w2all.at[slot, pl.ds(14 * j, 14 - j)]
+
+    def around(item, k):
+        ref = half_of(item, flip[k], k - 1)
+        sem = 3 * (k - 1)
+        return pltpu.make_async_remote_copy(
+            ref, ref, ssem.at[item, sem], rsem.at[item, sem],
+            device_id={"dp": flip[3 - k] * 2 + core}, device_id_type=MESH,
+        )
+
+    def sib_from(item, k):
+        chip = q if k == 0 else 3 - q if k == 3 else flip[k]
+        src, dst = ends(item, chip * 2 + core)
+        return pltpu.make_async_remote_copy(
+            src if k == 0 else dst, dst, fssem.at[item, k], frsem.at[item, k],
+            device_id={"dp": sib}, device_id_type=MESH,
+        )
+
+    def core_copy(item, k):
+        return sib_from(item, k) if crosses(item) else to_sib(item, k)
+
     def send(item):
-        for k in range(1, n):
-            to_peer(item, k).start()
-        to_sib(item, 0).start()
+        if crosses(item):
+            for k in (1, 2):
+                straight(item, k).start()
+        else:
+            for k in range(1, n):
+                to_peer(item, k).start()
+        core_copy(item, 0).start()
 
     def forward(item):
-        for k in range(1, n):
-            to_peer(item, k).wait_recv()
-            to_sib(item, k).start()
+        if crosses(item):
+            for k in (1, 2):
+                straight(item, k).wait_recv()
+                around(item, k).start()
+                core_copy(item, k).start()
+        else:
+            for k in range(1, n):
+                to_peer(item, k).wait_recv()
+                core_copy(item, k).start()
+
+    def across(item):
+        if crosses(item):
+            for k in (1, 2):
+                around(item, k).wait_recv()
+            core_copy(item, 3).start()
 
     def settle(item):
         for k in range(n):
-            to_sib(item, k).wait_recv()
+            core_copy(item, k).wait_recv()
 
     def to_mate():
         return pltpu.make_async_remote_copy(
@@ -122,15 +186,22 @@
         vol_halo(0).start()
         vol_halo(1).start()
 
-    for item in (0, 3, 1, 2):
+    for item in (0, 3, 1):
         send(item)
 
-    gat[me] = w1[:, :, lanes]
-    m1all[me] = m1[...]
-    w2all[me] = w2[...]
-    m2all[me] = m2[...]
-    volx[pl.ds(2 * h, 2)] = vol[...]
-
+    owned = [
+        pltpu.make_async_copy(src, dst, own.at[i])
+        for i, (src, dst) in enumerate((
+            (vol, volx.at[pl.ds(2 * h, 2)]),
+            (w1.at[:, :, lanes], gat.at[me]),
+            (m1, m1all.at[me]),
+            (w2, w2all.at[me]),
+            (m2, m2all.at[me]),
+        ))
+    ]
+    for copy in owned:
+        copy.start()
+    owned[0].wait()
     to_mate().wait_recv()
 
     @pl.when(takes)
@@ -157,14 +228,12 @@
             device_id={"space": mate}, device_id_type=MESH,
         )
 
-    def conv_phase(p):
-        acc = None
-        for t, sh in taps_of(p // 4, p // 2 % 2, p % 2):
-            w = gat[:, t].reshape(-1, 128)
-            term = jnp.dot(xs[sh], w, preferred_element_type=F32)
-            acc = term if acc is None else acc + term
-        act_all[p] = silu(acc).astype(BF).reshape(2, 128, 128)
-        to_act(p).start()
+    def conv_pair(pd, pr):
+        weight = lambda t: gat[:, t].reshape(-1, 128)
+        for pc, acc in enumerate(pair_sum(xs, weight, pd, pr)):
+            p = pd * 4 + pr * 2 + pc
+            act_all[p] = silu(acc).astype(BF).reshape(2, 128, 128)
+            to_act(p).start()
 
     def mix_phase(p):
         pd, pr, pc = p // 4, p // 2 % 2, p % 2
@@ -180,14 +249,20 @@
                     ]
 
     forward(0)
-    forward(3)
+    send(2)
+    across(0)
+    for copy in owned[1:]:
+        copy.wait()
+    forward(1)
     settle(0)
-    for p in range(4):
-        conv_phase(p)
-    forward(1)
+    conv_pair(0, 0)
+    conv_pair(0, 1)
     forward(2)
     send(4)
     send(5)
+    forward(3)
+    across(1)
+    across(2)
     settle(3)
     m1s[...] = m1all[...].reshape(2, 128, 256)
     for p in range(4):
@@ -211,8 +286,8 @@
 
     settle(1)
     settle(2)
-    for p in range(4, 8):
-        conv_phase(p)
+    conv_pair(1, 0)
+    conv_pair(1, 1)
     forward(4)
     forward(5)
     for p in range(4, 8):
@@ -232,13 +307,19 @@
         up_halo().wait_recv()
         up[4, 0:16] = halo[...]
 
+    across(4)
     settle(4)
     settle(5)
     for item in range(6):
         for k in range(n):
-            if k:
+            core_copy(item, k).wait_send()
+        if crosses(item):
+            for k in (1, 2):
+                straight(item, k).wait_send()
+                around(item, k).wait_send()
+        else:
+            for k in range(1, n):
                 to_peer(item, k).wait_send()
-            to_sib(item, k).wait_send()
     to_mate().wait_send()
     for p in range(8):
         to_act(p).wait_send()
@@ -262,16 +343,22 @@
         for sr in range(2):
             xs[sd * 4 + sr * 2] = x[sr : sr + 16].reshape(256, 256)
             xs[sd * 4 + sr * 2 + 1] = moved[sr : sr + 16].reshape(256, 256)
-    mixing = m2[...].reshape(128, 128)
-    for p in range(8):
-        pd, pr, pc = p // 4, p // 2 % 2, p % 2
-        acc = None
-        for t, sh in taps_of(pd, pr, pc):
-            term = jnp.dot(xs[sh], w2[:, t].reshape(256, 128), preferred_element_type=F32)
-            acc = term if acc is None else acc + term
-        r = jnp.dot(silu(acc).astype(BF), mixing, preferred_element_type=F32)
-        for i in range(16):
-            wide[pd, 2 * i + pr, pl.ds(pc, 16, stride=2), :] = r[i * 16 : i * 16 + 16]
+    m = m2[...].reshape(128, 128)
+    none = jnp.zeros_like(m)
+    mixing = jnp.concatenate(
+        [jnp.concatenate([m, none], 1), jnp.concatenate([none, m], 1)], 0
+    )
+    for pd in range(2):
+        for pr in range(2):
+            acc = jnp.concatenate(
+                pair_sum(xs, lambda t: w2[:, t].reshape(256, 128), pd, pr), 1
+            )
+            r = jnp.dot(silu(acc).astype(BF), mixing, preferred_element_type=F32)
+            for pc in range(2):
+                for i in range(16):
+                    wide[pd, 2 * i + pr, pl.ds(pc, 16, stride=2), :] = r[
+                        i * 16 : i * 16 + 16, pc * 128 : pc * 128 + 128
+                    ]
     out[...] = wide[...].astype(BF)
 
 
@@ -288,7 +375,7 @@
             jax.ShapeDtypeStruct((n_dp,) + w2.shape, BF),
             jax.ShapeDtypeStruct((n_dp,) + mix_two.shape, BF),
         ),
-        in_specs=[vm] * 5,
+        in_specs=[pl.BlockSpec(memory_space=pltpu.HBM)] * 5,
         out_specs=(vm,) * 3,
         scratch_shapes=[
             pltpu.VMEM((n_dp, 27, w1.shape[1], 128), BF),
@@ -303,7 +390,7 @@
             pltpu.VMEM((16, 16, 256), BF),
             dma((6, n)), dma((6, n)), dma((6, n)), dma((6, n)),
             dma((1,)), dma((1,)), dma((2,)), dma((1,)),
-            dma((8,)), dma((8,)), dma((1,)), dma((1,)),
+            dma((8,)), dma((8,)), dma((1,)), dma((1,)), dma((5,)),
         ],
         compiler_params=pltpu.CompilerParams(
             collective_id=0, has_side_effects=True, vmem_limit_bytes=48 * 2**20

time: 54.4 us -> 45 us (0.83)
  Pallas kernels: 49.7 us -> 40.3 us
    pallas_call x1, Pallas kernels: 39.9 us -> 33.8 us  [per_device(): pl.pallas_call(functools.partial(first_kernel, n_dp, n_space), out_shape=...]
    pallas_call x1, Pallas kernels: 9.74 us -> 6.48 us  [per_device(): pl.pallas_call(second_kernel, grid=(4,), out_shape=jax.ShapeDtypeStruct((...]
where the time goes in v2:
time: 45 us; the launch traced here: 44.7 us
  Pallas kernels  40.3 us (90%)
  local copies, waits for them, and re-layouts  4.41 us (10%)
    pallas_call x1, Pallas kernels, per_device(): pl.pallas_call(functools.partial(first_kernel, n_dp, n_space), out_shape=...  33.8 us
    pallas_call x1, Pallas kernels, per_device(): pl.pallas_call(second_kernel, grid=(4,), out_shape=jax.ShapeDtypeStruct((...  6.48 us
    unnamed x10, local copies, waits for them, and re-layouts  4.41 us

profile of v2, /device:TPU:1, one launch (start us, length us, event | category | flops | bytes accessed | tf_op | source)
XLA Modules:
  0.0 44.7 jit_solution(1194912015810405612)
XLA Ops:
  0.0 0.0 copy-start
  0.0 1.2 %copy-done = bf16[3,3,3,64,256]{4,3,2,1,0:T(8,128)(2,1)S(1)} copy-done((bf16[3,3,3,64,256]{4,3,2,1,0:T(8,128)(2,1)S(1)}, bf16[3,3,3,64,256]{4,3,2,1,0:T(8,128)(2,1)}, u32[]{:S(2)}) %copy-start) | copy-done | bytes 884760
  1.2 0.0 copy-start.1
  1.2 0.9 %copy-done.1 = bf16[3,3,3,32,128]{4,3,2,1,0:T(8,128)(2,1)S(1)} copy-done((bf16[3,3,3,32,128]{4,3,2,1,0:T(8,128)(2,1)S(1)}, bf16[3,3,3,32,128]{4,3,2,1,0:T(8,128)(2,1)}, u32[]{:S(2)}) %copy-start.1) | copy-done | bytes 221208
  2.1 0.0 copy-start.2
  2.1 0.9 %copy-done.2 = bf16[1,2,8,8,512]{4,3,2,1,0:T(8,128)(2,1)S(1)} copy-done((bf16[1,2,8,8,512]{4,3,2,1,0:T(8,128)(2,1)S(1)}, bf16[1,2,8,8,512]{4,3,2,1,0:T(8,128)(2,1)}, u32[]{:S(2)}) %copy-start.2) | copy-done | bytes 131096
  3.0 0.0 copy-start.3
  3.0 0.7 %copy-done.3 = bf16[32,256]{1,0:T(8,128)(2,1)S(1)} copy-done((bf16[32,256]{1,0:T(8,128)(2,1)S(1)}, bf16[32,256]{1,0:T(8,128)(2,1)}, u32[]{:S(2)}) %copy-start.3) | copy-done | bytes 16408
  3.7 0.0 copy-start.4
  3.7 0.7 %copy-done.4 = bf16[16,128]{1,0:T(8,128)(2,1)S(1)} copy-done((bf16[16,128]{1,0:T(8,128)(2,1)S(1)}, bf16[16,128]{1,0:T(8,128)(2,1)}, u32[]{:S(2)}) %copy-start.4) | copy-done | bytes 4120
  4.4 33.8 %shard_map.55 = (bf16[5,17,16,256]{3,2,1,0:T(8,128)(2,1)S(1)}, bf16[8,27,32,128]{3,2,1,0:T(8,128)(2,1)S(1)}, bf16[8,16,128]{2,1,0:T(8,128)(2,1)S(1)}) custom-call(bf16[2,8,8,512]{3,2,1,0:T(8,128)(2,1)S(1)} %bitcast.6, bf16[27,64,256]{2,1,0:T(8,128)(2,1)S(1)} %bitcast.4, bf16[32,256]{1,0:T(8,128)(2,1)S(1)} %copy-done.3, bf16[27,32,128]{2,1,0:T(8,128)(2,1)S(1)} %bitcast.5, ...), custom_call_target="tpu_custom_call" | custom-call | tf_op jit(solution)/shard_map/pallas_call | solution.py:371
  38.2 6.5 %shard_map.56 = bf16[8,32,32,128]{3,2,1,0:T(8,128)(2,1)} custom-call(bf16[5,17,16,256]{3,2,1,0:T(8,128)(2,1)S(1)} %get-tuple-element.8.up, bf16[8,27,32,128]{3,2,1,0:T(8,128)(2,1)S(1)} %get-tuple-element.9.w2, bf16[8,16,128]{2,1,0:T(8,128)(2,1)S(1)} %get-tuple-element.10.m2), custom_call_target="tpu_custom_call" | custom-call | tf_op jit(solution)/shard_map/pallas_call | solution.py:400
Async XLA Ops:
  0.0 1.2 %copy-start = (bf16[3,3,3,64,256]{4,3,2,1,0:T(8,128)(2,1)S(1)}, bf16[3,3,3,64,256]{4,3,2,1,0:T(8,128)(2,1)}, u32[]{:S(2)}) copy-start(bf16[3,3,3,64,256]{4,3,2,1,0:T(8,128)(2,1)} %param.6) | copy-start | bytes 2654212
  1.2 0.9 %copy-start.1 = (bf16[3,3,3,32,128]{4,3,2,1,0:T(8,128)(2,1)S(1)}, bf16[3,3,3,32,128]{4,3,2,1,0:T(8,128)(2,1)}, u32[]{:S(2)}) copy-start(bf16[3,3,3,32,128]{4,3,2,1,0:T(8,128)(2,1)} %param.8) | copy-start | bytes 663556
  2.1 0.9 %copy-start.2 = (bf16[1,2,8,8,512]{4,3,2,1,0:T(8,128)(2,1)S(1)}, bf16[1,2,8,8,512]{4,3,2,1,0:T(8,128)(2,1)}, u32[]{:S(2)}) copy-start(bf16[1,2,8,8,512]{4,3,2,1,0:T(8,128)(2,1)} %param.5) | copy-start | bytes 393220
  3.0 0.7 %copy-start.3 = (bf16[32,256]{1,0:T(8,128)(2,1)S(1)}, bf16[32,256]{1,0:T(8,128)(2,1)}, u32[]{:S(2)}) copy-start(bf16[32,256]{1,0:T(8,128)(2,1)} %m1.1) | copy-start | bytes 49156
  3.7 0.7 %copy-start.4 = (bf16[16,128]{1,0:T(8,128)(2,1)S(1)}, bf16[16,128]{1,0:T(8,128)(2,1)}, u32[]{:S(2)}) copy-start(bf16[16,128]{1,0:T(8,128)(2,1)} %m2.1) | copy-start | bytes 12292

commit v3 on v2

--- a/solution.py
+++ b/solution.py
@@ -32,11 +32,11 @@
     return both[:, :128], both[:, 128:] + extra
 
 
-def first_kernel(
+def fused_kernel(
     n_dp, n_space, vol, w1, m1, w2, m2,
-    up, w2all, m2all,
-    gat, m1all, m1s, volx, pad, xs, act_all, act_in, upf, halo,
-    ssem, rsem, fssem, frsem, vs, vr, hs, hr, asem, arsem, us, ur, own,
+    decoded,
+    up, w2all, m2all, wide, views, planes, gat, m1all, m1s, volx, pad, xs, act_all, act_in, upf, halo,
+    ssem, rsem, fssem, frsem, vs, vr, hs, hr, asem, arsem, us, ur, own, outsem,
 ):
     n = n_dp // 2
     me = lax.axis_index("dp")
@@ -310,6 +310,17 @@
     across(4)
     settle(4)
     settle(5)
+
+    def to_decoded(d):
+        return pltpu.make_async_copy(
+            planes.at[d], decoded.at[pl.ds(2 * d, 2)], outsem.at[d]
+        )
+
+    @pl.loop(0, 4)
+    def _(d):
+        second_block(d, up, w2all, m2all, planes.at[d], wide, views)
+        to_decoded(d).start()
+
     for item in range(6):
         for k in range(n):
             core_copy(item, k).wait_send()
@@ -333,9 +344,11 @@
     def _():
         up_halo().wait_send()
 
-
-def second_kernel(up, w2, m2, out, wide, xs):
-    d = pl.program_id(0)
+    for d in range(4):
+        to_decoded(d).wait()
+
+
+def second_block(d, up, w2, m2, out, wide, xs):
     for sd in range(2):
         x = up[d + sd]
         moved = x.astype(F32)
@@ -366,18 +379,20 @@
     n = n_dp // 2
     w1 = conv_one.reshape((27,) + conv_one.shape[3:])
     w2 = conv_two.reshape((27,) + conv_two.shape[3:])
-    vm = pl.BlockSpec(memory_space=pltpu.VMEM)
+    hbm = pl.BlockSpec(memory_space=pltpu.HBM)
     dma = pltpu.SemaphoreType.DMA
-    up, w2all, m2all = pl.pallas_call(
-        functools.partial(first_kernel, n_dp, n_space),
-        out_shape=(
-            jax.ShapeDtypeStruct((5, 17, 16, 256), BF),
-            jax.ShapeDtypeStruct((n_dp,) + w2.shape, BF),
-            jax.ShapeDtypeStruct((n_dp,) + mix_two.shape, BF),
-        ),
-        in_specs=[pl.BlockSpec(memory_space=pltpu.HBM)] * 5,
-        out_specs=(vm,) * 3,
+    decoded = pl.pallas_call(
+        functools.partial(fused_kernel, n_dp, n_space),
+        out_shape=jax.ShapeDtypeStruct((8, 32, 32, 128), BF),
+        in_specs=[hbm] * 5,
+        out_specs=hbm,
         scratch_shapes=[
+            pltpu.VMEM((5, 17, 16, 256), BF),
+            pltpu.VMEM((n_dp,) + w2.shape, BF),
+            pltpu.VMEM((n_dp,) + mix_two.shape, BF),
+            pltpu.VMEM((2, 32, 32, 128), F32),
+            pltpu.VMEM((8, 256, 256), BF),
+            pltpu.VMEM((4, 2, 32, 32, 128), BF),
             pltpu.VMEM((n_dp, 27, w1.shape[1], 128), BF),
             pltpu.VMEM((n_dp,) + mix_one.shape, BF),
             pltpu.VMEM((2, 128, 256), BF),
@@ -390,22 +405,12 @@
             pltpu.VMEM((16, 16, 256), BF),
             dma((6, n)), dma((6, n)), dma((6, n)), dma((6, n)),
             dma((1,)), dma((1,)), dma((2,)), dma((1,)),
-            dma((8,)), dma((8,)), dma((1,)), dma((1,)), dma((5,)),
+            dma((8,)), dma((8,)), dma((1,)), dma((1,)), dma((5,)), dma((4,)),
         ],
         compiler_params=pltpu.CompilerParams(
-            collective_id=0, has_side_effects=True, vmem_limit_bytes=48 * 2**20
+            collective_id=0, has_side_effects=True, vmem_limit_bytes=60 * 2**20
         ),
     )(volume[0], w1, mix_one, w2, mix_two)
-    whole = lambda shape: pl.BlockSpec(shape, lambda d: (0,) * len(shape))
-    decoded = pl.pallas_call(
-        second_kernel,
-        grid=(4,),
-        out_shape=jax.ShapeDtypeStruct((8, 32, 32, 128), BF),
-        in_specs=[whole(up.shape), whole(w2all.shape), whole(m2all.shape)],
-        out_specs=pl.BlockSpec((2, 32, 32, 128), lambda d: (d, 0, 0, 0)),
-        scratch_shapes=[pltpu.VMEM((2, 32, 32, 128), F32), pltpu.VMEM((8, 256, 256), BF)],
-        compiler_params=pltpu.CompilerParams(vmem_limit_bytes=40 * 2**20),
-    )(up, w2all, m2all)
     return decoded[None]
 
 

time: 45 us -> 43.9 us (0.976)
  local copies, waits for them, and re-layouts: 4.41 us -> 3.27 us
    unnamed x10 -> x1, local copies, waits for them, and re-layouts: 4.41 us -> 3.27 us
    pallas_call x2 -> x1, Pallas kernels: 40.3 us -> 40.4 us  [per_device(): pl.pallas_call(functools.partial(fused_kernel, n_dp, n_space), out_shape=...]
where the time goes in v3:
time: 43.9 us; the launch traced here: 43.7 us
  Pallas kernels  40.4 us (92%)
  local copies, waits for them, and re-layouts  3.27 us (7%)
    pallas_call x1, Pallas kernels, per_device(): pl.pallas_call(functools.partial(fused_kernel, n_dp, n_space), out_shape=...  40.4 us
    unnamed x1, local copies, waits for them, and re-layouts  3.27 us

profile of v3, /device:TPU:1, one launch (start us, length us, event | category | flops | bytes accessed | tf_op | source)
XLA Modules:
  0.0 43.7 jit_solution(14526318710118266931)
XLA Ops:
  0.0 40.4 %shard_map.55 = bf16[8,32,32,128]{3,2,1,0:T(8,128)(2,1)} custom-call(bf16[2,8,8,512]{3,2,1,0:T(8,128)(2,1)} %bitcast.7, bf16[27,64,256]{2,1,0:T(8,128)(2,1)} %bitcast.5, bf16[32,256]{1,0:T(8,128)(2,1)} %m1.1, bf16[27,32,128]{2,1,0:T(8,128)(2,1)} %bitcast.6, bf16[16,128]{1,0:T(8,128)(2,1)} %m2.1), custom_call_target="tpu_custom_call" | custom-call | tf_op jit(solution)/shard_map/pallas_call | solution.py:384
  40.5 3.3 %copy.7 = bf16[1,8,32,32,128]{4,3,2,1,0:T(8,128)(2,1)} copy(bf16[1,8,32,32,128]{4,3,2,1,0:T(8,128)(2,1)} %bitcast.4) | data formatting | bytes 4194304

commit v4 on v3

--- a/solution.py
+++ b/solution.py
@@ -313,10 +313,10 @@
 
     def to_decoded(d):
         return pltpu.make_async_copy(
-            planes.at[d], decoded.at[pl.ds(2 * d, 2)], outsem.at[d]
-        )
-
-    @pl.loop(0, 4)
+            planes.at[d], decoded.at[pl.ds(4 * d, 4)], outsem.at[d]
+        )
+
+    @pl.loop(0, 2)
     def _(d):
         second_block(d, up, w2all, m2all, planes.at[d], wide, views)
         to_decoded(d).start()
@@ -344,18 +344,18 @@
     def _():
         up_halo().wait_send()
 
-    for d in range(4):
+    for d in range(2):
         to_decoded(d).wait()
 
 
 def second_block(d, up, w2, m2, out, wide, xs):
     for sd in range(2):
-        x = up[d + sd]
+        x = up[pl.ds(2 * d + sd, 2)]
         moved = x.astype(F32)
-        moved = jnp.concatenate([moved[:, 1:], jnp.zeros_like(moved[:, :1])], 1).astype(BF)
+        moved = jnp.concatenate([moved[:, :, 1:], jnp.zeros_like(moved[:, :, :1])], 2).astype(BF)
         for sr in range(2):
-            xs[sd * 4 + sr * 2] = x[sr : sr + 16].reshape(256, 256)
-            xs[sd * 4 + sr * 2 + 1] = moved[sr : sr + 16].reshape(256, 256)
+            xs[sd * 4 + sr * 2] = x[:, sr : sr + 16].reshape(512, 256)
+            xs[sd * 4 + sr * 2 + 1] = moved[:, sr : sr + 16].reshape(512, 256)
     m = m2[...].reshape(128, 128)
     none = jnp.zeros_like(m)
     mixing = jnp.concatenate(
@@ -368,8 +368,8 @@
             )
             r = jnp.dot(silu(acc).astype(BF), mixing, preferred_element_type=F32)
             for pc in range(2):
-                for i in range(16):
-                    wide[pd, 2 * i + pr, pl.ds(pc, 16, stride=2), :] = r[
+                for i in range(32):
+                    wide[i // 16 * 2 + pd, i % 16 * 2 + pr, pl.ds(pc, 16, stride=2), :] = r[
                         i * 16 : i * 16 + 16, pc * 128 : pc * 128 + 128
                     ]
     out[...] = wide[...].astype(BF)
@@ -390,9 +390,9 @@
             pltpu.VMEM((5, 17, 16, 256), BF),
             pltpu.VMEM((n_dp,) + w2.shape, BF),
             pltpu.VMEM((n_dp,) + mix_two.shape, BF),
-            pltpu.VMEM((2, 32, 32, 128), F32),
-            pltpu.VMEM((8, 256, 256), BF),
-            pltpu.VMEM((4, 2, 32, 32, 128), BF),
+            pltpu.VMEM((4, 32, 32, 128), F32),
+            pltpu.VMEM((8, 512, 256), BF),
+            pltpu.VMEM((2, 4, 32, 32, 128), BF),
             pltpu.VMEM((n_dp, 27, w1.shape[1], 128), BF),
             pltpu.VMEM((n_dp,) + mix_one.shape, BF),
             pltpu.VMEM((2, 128, 256), BF),
@@ -405,7 +405,7 @@
             pltpu.VMEM((16, 16, 256), BF),
             dma((6, n)), dma((6, n)), dma((6, n)), dma((6, n)),
             dma((1,)), dma((1,)), dma((2,)), dma((1,)),
-            dma((8,)), dma((8,)), dma((1,)), dma((1,)), dma((5,)), dma((4,)),
+            dma((8,)), dma((8,)), dma((1,)), dma((1,)), dma((5,)), dma((2,)),
         ],
         compiler_params=pltpu.CompilerParams(
             collective_id=0, has_side_effects=True, vmem_limit_bytes=60 * 2**20

time: 43.9 us -> 42.8 us (0.975)
  Pallas kernels: 40.4 us -> 39.3 us
    pallas_call x1, Pallas kernels: 40.4 us -> 39.3 us  [per_device(): pl.pallas_call(functools.partial(fused_kernel, n_dp, n_space), out_shape=...]
where the time goes in v4:
time: 42.8 us; the launch traced here: 42.6 us
  Pallas kernels  39.3 us (92%)
  local copies, waits for them, and re-layouts  3.27 us (8%)
    pallas_call x1, Pallas kernels, per_device(): pl.pallas_call(functools.partial(fused_kernel, n_dp, n_space), out_shape=...  39.3 us
    unnamed x1, local copies, waits for them, and re-layouts  3.27 us

profile of v4, /device:TPU:1, one launch (start us, length us, event | category | flops | bytes accessed | tf_op | source)
XLA Modules:
  0.0 42.6 jit_solution(13711145262894186903)
XLA Ops:
  0.0 39.3 %shard_map.55 = bf16[8,32,32,128]{3,2,1,0:T(8,128)(2,1)} custom-call(bf16[2,8,8,512]{3,2,1,0:T(8,128)(2,1)} %bitcast.7, bf16[27,64,256]{2,1,0:T(8,128)(2,1)} %bitcast.5, bf16[32,256]{1,0:T(8,128)(2,1)} %m1.1, bf16[27,32,128]{2,1,0:T(8,128)(2,1)} %bitcast.6, bf16[16,128]{1,0:T(8,128)(2,1)} %m2.1), custom_call_target="tpu_custom_call" | custom-call | tf_op jit(solution)/shard_map/pallas_call | solution.py:384
  39.3 3.3 %copy.7 = bf16[1,8,32,32,128]{4,3,2,1,0:T(8,128)(2,1)} copy(bf16[1,8,32,32,128]{4,3,2,1,0:T(8,128)(2,1)} %bitcast.4) | data formatting | bytes 4194304

commit v5 on v4

--- a/solution.py
+++ b/solution.py
@@ -60,11 +60,18 @@
     for k in range(1, n):
         pl.semaphore_signal(barrier, inc=1, device_id={"dp": peer(k)}, device_id_type=MESH)
     pl.semaphore_signal(barrier, inc=1, device_id={"dp": sib}, device_id_type=MESH)
-    for k in range(1, n_space):
-        pl.semaphore_signal(
-            barrier, inc=1, device_id={"space": lax.rem(s + k, n_space)}, device_id_type=MESH
-        )
-    pl.semaphore_wait(barrier, n + n_space - 1)
+    greeted = n
+    for k in (-2, -1, 1, 2):
+        there = jnp.logical_and(s + k >= 0, s + k < n_space)
+        greeted = greeted + there.astype(jnp.int32)
+
+        @pl.when(there)
+        def _(k=k):
+            pl.semaphore_signal(
+                barrier, inc=1, device_id={"space": s + k}, device_id_type=MESH
+            )
+
+    pl.semaphore_wait(barrier, greeted)
 
     lanes = pl.ds(pl.multiple_of(h * 128, 128), 128)
 

time: 42.8 us -> 42.8 us (level)
  no operation moved by 1% of the time
where the time goes in v5:
time: 42.8 us; the launch traced here: 42.6 us
  Pallas kernels  39.3 us (92%)
  local copies, waits for them, and re-layouts  3.27 us (8%)
    pallas_call x1, Pallas kernels, per_device(): pl.pallas_call(functools.partial(fused_kernel, n_dp, n_space), out_shape=...  39.3 us
    unnamed x1, local copies, waits for them, and re-layouts  3.27 us

profile of v5, /device:TPU:1, one launch (start us, length us, event | category | flops | bytes accessed | tf_op | source)
XLA Modules:
  0.0 42.6 jit_solution(2530350589576977232)
XLA Ops:
  0.0 39.3 %shard_map.55 = bf16[8,32,32,128]{3,2,1,0:T(8,128)(2,1)} custom-call(bf16[2,8,8,512]{3,2,1,0:T(8,128)(2,1)} %bitcast.7, bf16[27,64,256]{2,1,0:T(8,128)(2,1)} %bitcast.5, bf16[32,256]{1,0:T(8,128)(2,1)} %m1.1, bf16[27,32,128]{2,1,0:T(8,128)(2,1)} %bitcast.6, bf16[16,128]{1,0:T(8,128)(2,1)} %m2.1), custom_call_target="tpu_custom_call" | custom-call | tf_op jit(solution)/shard_map/pallas_call | solution.py:391
  39.4 3.3 %copy.7 = bf16[1,8,32,32,128]{4,3,2,1,0:T(8,128)(2,1)} copy(bf16[1,8,32,32,128]{4,3,2,1,0:T(8,128)(2,1)} %bitcast.4) | data formatting | bytes 4194304
